TPU v7x, 128 devices: a whole 4x4x4 slice. The times are simulated.
128 devices in a mesh: dp: 16 (over z, y), expert: 8 (over x, core).
Axes of the slice: x: 4, y: 4, z: 4, core: 2. Of those that a mesh axis runs over, the one named last changes fastest.
Arguments:
- hidden: bfloat16 [8, 1024, 8192], P('expert', None, 'dp'), may hold values from -6 to 6
- down_weight: bfloat16 [8, 8192, 6144], P('expert', 'dp'), may hold values from -0.0625 to 0.0625
- grad_out: bfloat16 [2048, 6144], P('dp', 'expert'), may hold values from -2 to 2
- routing: int32 [2048, 2], P('dp'), may hold values from 0 to 7, all different within a row; in each aligned block of 128 rows (0 to 127, 128 to 255, ...) at most 64 rows name the same one
- gates: float32 [2048, 2], P('dp'), may hold values from 0.25 to 1
Outputs:
- mixed_out: bfloat16 [2048, 6144], P('dp', 'expert')
- grad_hidden: bfloat16 [8, 1024, 8192], P('expert', None, 'dp')
- grad_weight: bfloat16 [8, 8192, 6144], P('expert', 'dp')
Inputs may be any that keep to these rules, and one draw needn't show every extreme that they name: `routing`: among the 128 tokens of one sequence shard (aligned blocks of rows), each expert is named by at most 64 tokens, a bound that some block reaches; a token names 2 different experts.
All inputs are finite; a program needn't handle non-finite values.
Results may differ from a plain program's by a relative error of at most 0.017.
Values may be sent and summed in bfloat16 or wider, within the bound.
A program may use at most 128 MiB of HBM per device.

v0:
```python
import jax
import jax.numpy as jnp
from jax import lax
from jax.sharding import PartitionSpec as P


def dispatch_weights(routing, gates, experts, capacity):
    flattened = routing.reshape(-1)
    onehot = (flattened[:, None] == jnp.arange(experts, dtype=jnp.int32)[None, :]).astype(jnp.int32)
    position = jnp.sum((jnp.cumsum(onehot, axis=0) - onehot) * onehot, axis=1)
    target = flattened * capacity + position
    picked = (jnp.arange(experts * capacity, dtype=jnp.int32)[:, None] == target[None, :]).astype(
        jnp.float32
    )
    picked = picked * gates.reshape(-1)[None, :]
    return jnp.sum(picked.reshape(experts * capacity, routing.shape[0], routing.shape[1]), axis=2)


def body(hidden, down_weight, grad_out, routing, gates):
    highest = lax.Precision.HIGHEST
    groups = lax.axis_size("dp")
    owners = lax.axis_size("expert")
    experts = hidden.shape[0] * owners
    slot_total = hidden.shape[1]
    capacity = slot_total // groups
    dispatch = dispatch_weights(routing, gates, experts, capacity)
    hidden_rows = hidden[0]
    weight = down_weight[0]
    own_rows = lax.psum_scatter(
        jnp.dot(hidden_rows, weight, preferred_element_type=jnp.float32).astype(jnp.bfloat16),
        "dp",
        scatter_dimension=0,
        tiled=True,
    ).astype(jnp.float32)
    own_rows = own_rows.astype(jnp.bfloat16)[None]
    outputs = lax.all_to_all(own_rows, "expert", split_axis=2, concat_axis=0, tiled=True)
    flat_outputs = outputs.reshape(experts * capacity, outputs.shape[-1]).astype(jnp.float32)
    mixed_out = lax.dot_general(dispatch, flat_outputs, (((0,), (0,)), ((), ())), precision=highest)
    mixed_out = mixed_out.astype(jnp.bfloat16)
    routed = jnp.dot(dispatch, grad_out.astype(jnp.float32), precision=highest).astype(jnp.bfloat16)
    routed = routed.reshape(experts, capacity, routed.shape[-1])
    shards = lax.all_gather(routed, "dp", axis=1, tiled=True)
    gathered = lax.all_to_all(shards, "expert", split_axis=0, concat_axis=2, tiled=True)
    grad_rows = gathered[0]
    hidden_acc = lax.dot_general(
        grad_rows, weight, (((1,), (1,)), ((), ())), preferred_element_type=jnp.float32
    )
    weight_acc = lax.dot_general(
        hidden_rows, grad_rows, (((0,), (0,)), ((), ())), preferred_element_type=jnp.float32
    )
    grad_hidden = hidden_acc.astype(jnp.bfloat16)[None]
    grad_weight = weight_acc.astype(jnp.bfloat16)[None]
    return (mixed_out, grad_hidden, grad_weight)


def solution(mesh):
    return jax.shard_map(
        body,
        mesh=mesh,
        in_specs=(
            P("expert", None, "dp"),
            P("expert", "dp", None),
            P("dp", "expert"),
            P("dp", None),
            P("dp", None),
        ),
        out_specs=(P("dp", "expert"), P("expert", None, "dp"), P("expert", "dp", None)),
        check_vma=False,
    )
```

profile of v0, /device:TPU:1, one launch (start us, length us, event | category | flops | bytes accessed | tf_op | source)
XLA Modules:
  0.0 412.6 jit_solution(2753633807053152809)
XLA Ops:
  7.2 1.2 copy-done
  8.4 12.3 %convolution_convert_fusion = bf16[1024,6144]{1,0:T(8,128)(2,1)} fusion(bf16[1,512,6144]{2,1,0:T(8,128)(2,1)} %param.6, bf16[1,1024,512]{2,1,0:T(8,128)(2,1)S(1)} %copy-done), kind=kOutput, calls=%fused_computation | convolution fusion | flops 6448742400 | bytes 19922944 | tf_op jit(solution)/shard_map/dot_general | solution.py:30
  20.7 0.6 copy-done.2
  21.3 0.1 copy.50
  21.5 0.1 eq.44
  21.6 0.1 eq.40
  21.8 0.6 reduce-window.6
  22.3 0.2 slice_reduce_fusion
  22.6 0.1 fusion.13
  22.7 0.1 reduce_sum.21
  22.8 0.1 copy.52
  22.9 0.1 select_reduce_fusion
  23.0 0.8 convolution_convert_fusion.2
  23.8 1.3 copy.56
  25.1 93.8 %reduce-scatter.2.cloned.1.call-done = bf16[64,6144]{1,0:T(8,128)(2,1)} async-done(((bf16[1024,6144]{1,0:T(8,128)(2,1)}), bf16[64,6144]{1,0:T(8,128)(2,1)}) %reduce-scatter.2.cloned.1.call-update) | async-done | bytes 786448 | tf_op jit(solution)/shard_map/reduce_scatter | solution.py:29
  118.9 7.2 %copy.53 = bf16[1,64,6144]{1,0,2:T(2,128)(2,1)} copy(bf16[1,64,6144]{2,1,0:T(8,128)(2,1)} %bitcast.58) | data formatting | bytes 1572864 | tf_op jit(solution)/shard_map/broadcast_in_dim | solution.py:35
  126.1 0.5 broadcast.37
  126.6 34.3 %reduce.2 = bf16[6144,64]{1,0:T(8,128)(2,1)S(1)} reduce(bf16[6144,1,64]{2,1,0:T(2,128)(2,1)} %bitcast.52, bf16[]{:T(256)} %broadcast.37), dimensions={1}, to_apply=%bitcast.43.reduce_sub_computation | reduce | bytes 1572866
  161.0 1.9 reshape.59
  162.9 5.4 %all-to-all-start = ((bf16[8,2,24576]{2,1,0:T(2,128)(2,1)}), bf16[8,2,24576]{2,1,0:T(2,128)(2,1)S(1)}, u32[]{:S(2)}, u32[]{:S(2)}) async-start(bf16[8,2,24576]{2,1,0:T(2,128)(2,1)} %reshape.59), calls=%async_computation.1 | async-start | bytes 1572864 | tf_op jit(solution)/shard_map/all_to_all | solution.py:36
  168.3 41.9 %all-gather.2.cloned.1.call-done = bf16[8,1024,768]{2,0,1:T(8,128)(2,1)} async-done(((bf16[8,64,768]{2,0,1:T(8,128)(2,1)}), bf16[8,1024,768]{2,0,1:T(8,128)(2,1)}) %all-gather.2.cloned.1.call-update) | async-done | bytes 12582928 | tf_op jit(solution)/shard_map/all_gather | solution.py:42
  210.2 16.5 %copy.57 = bf16[8,1024,768]{1,2,0:T(8,128)(2,1)} copy(bf16[8,1024,768]{2,0,1:T(8,128)(2,1)} %all-gather.2.cloned.1.call-done) | data formatting | bytes 25165824 | tf_op jit(solution)/shard_map/all_gather | solution.py:42
  226.7 6.2 %all-to-all-start.1 = ((bf16[8,1024,768]{1,2,0:T(8,128)(2,1)}), bf16[8,1024,768]{1,2,0:T(8,128)(2,1)}, u32[]{:S(2)}, u32[]{:S(2)}) async-start(bf16[8,1024,768]{1,2,0:T(8,128)(2,1)} %copy.57), calls=%async_computation.2 | async-start | bytes 25165824 | tf_op jit(solution)/shard_map/all_to_all | solution.py:43
  232.9 3.9 reshape.60
  236.9 6.0 %copy.54 = bf16[1,64,6144]{2,1,0:T(8,128)(2,1)S(1)} copy(bf16[1,64,6144]{1,0,2:T(2,128)(2,1)} %bitcast.53) | data formatting | bytes 1572864 | tf_op jit(solution)/shard_map/all_to_all | solution.py:36
  242.9 0.1 copy.59
  243.1 0.1 copy.55
  243.3 1.2 convolution_convert_fusion.3
  244.5 127.1 %all-to-all-done.1 = bf16[8,1024,768]{1,2,0:T(8,128)(2,1)} async-done(((bf16[8,1024,768]{1,2,0:T(8,128)(2,1)}), bf16[8,1024,768]{1,2,0:T(8,128)(2,1)}, u32[]{:S(2)}, u32[]{:S(2)}) %all-to-all-start.1) | async-done | bytes 12582944 | tf_op jit(solution)/shard_map/all_to_all | solution.py:43
  371.6 12.4 %fusion.7 = bf16[1,1024,512]{2,1,0:T(8,128)(2,1)} fusion(bf16[1024,6144]{0,1:T(8,128)(2,1)} %bitcast.10, bf16[1,512,6144]{2,1,0:T(8,128)(2,1)} %param.6), kind=kOutput, calls=%fused_computation.8 | convolution fusion | flops 6442975232 | bytes 19922944 | tf_op jit(solution)/shard_map/dot_general | solution.py:45
  384.0 13.1 %fusion = bf16[1,512,6144]{1,2,0:T(8,128)(2,1)} fusion(bf16[1024,6144]{0,1:T(8,128)(2,1)} %bitcast.10, bf16[1,1024,512]{2,1,0:T(8,128)(2,1)S(1)} %copy-done), kind=kOutput, calls=%fused_computation.2 | convolution fusion | flops 6445596672 | bytes 19922944 | tf_op jit(solution)/shard_map/dot_general | solution.py:48
  397.2 8.6 %copy.58 = bf16[1,512,6144]{2,1,0:T(8,128)(2,1)} copy(bf16[1,512,6144]{1,2,0:T(8,128)(2,1)} %fusion) | data formatting | bytes 12582912
  (16 shorter events, 0.2 us)
Async XLA Ops:
  7.2 1.2 copy-start
  7.2 111.7 %reduce-scatter.2.cloned.1.call-start = ((), (), s32[]{:S(2)}) async-start(), calls=%async_computation.3 | async-start | bytes 13369344 | tf_op jit(solution)/shard_map/reduce_scatter | solution.py:29
  20.7 0.7 copy-start.2
  20.7 2.2 copy-start.3
  20.7 2.3 copy-start.1
  20.7 189.5 %all-gather.2.cloned.1.call-start = ((), (), s32[]{:S(2)}) async-start(), calls=%async_computation.4 | async-start | bytes 13369344 | tf_op jit(solution)/shard_map/all_gather | solution.py:42
  162.9 63.8 %all-to-all-start = ((bf16[8,2,24576]{2,1,0:T(2,128)(2,1)}), bf16[8,2,24576]{2,1,0:T(2,128)(2,1)S(1)}, u32[]{:S(2)}, u32[]{:S(2)}) async-start(bf16[8,2,24576]{2,1,0:T(2,128)(2,1)} %reshape.59), calls=%async_computation.1 | async-start | bytes 1572864 | tf_op jit(solution)/shard_map/all_to_all | solution.py:36
  226.7 144.9 %all-to-all-start.1 = ((bf16[8,1024,768]{1,2,0:T(8,128)(2,1)}), bf16[8,1024,768]{1,2,0:T(8,128)(2,1)}, u32[]{:S(2)}, u32[]{:S(2)}) async-start(bf16[8,1024,768]{1,2,0:T(8,128)(2,1)} %copy.57), calls=%async_computation.2 | async-start | bytes 25165824 | tf_op jit(solution)/shard_map/all_to_all | solution.py:43
Sparse Core Ops, SparseCore 0:
  20.8 98.0 reduce-scatter.1
  121.0 89.1 all-gather.1
where the time goes:
time: 414 us; the launch traced here: 413 us
  waiting for transfers between devices  263 us (64%)
  local copies, waits for them, and re-layouts  49 us (12%)
  matrix products  39.8 us (10%)
  other arithmetic  35.1 us (8%)
  between operations  14.1 us (3%)
  starting transfers between devices  11.7 us (3%)
    all_to_all x1, waiting for transfers between devices, body(): lax.all_to_all(shards, 'expert', split_axis=0, concat_axis=2, tiled=True)  127 us
    reduce_scatter x1, waiting for transfers between devices, body(): lax.psum_scatter(jnp.dot(hidden_rows, weight, preferred_element_type=jnp....  93.8 us
    all_gather x1, waiting for transfers between devices, body(): shards = lax.all_gather(routed, 'dp', axis=1, tiled=True)  41.9 us
    unnamed x1, other arithmetic  34.3 us
    unnamed x14, local copies, waits for them, and re-layouts  17 us
    all_gather x1, local copies, waits for them, and re-layouts, body(): shards = lax.all_gather(routed, 'dp', axis=1, tiled=True)  16.5 us
    dot_general x1, matrix products, body(): lax.dot_general(hidden_rows, grad_rows, (((0,), (0,)), ((), ())), preferr...  13.1 us
    dot_general x1, matrix products, body(): lax.dot_general(grad_rows, weight, (((1,), (1,)), ((), ())), preferred_el...  12.4 us
  transfers between devices with their start and end apart: 4, of which 3 were waited for; matrix products, arithmetic and copies ran while one was open for 18% of the time, Pallas kernels for 0%

commit v1 on v0

v1 whole, which is shorter than its diff:
```python
import jax
import jax.numpy as jnp
from jax import lax
from jax.experimental import pallas as pl
from jax.experimental.pallas import tpu as pltpu
from jax.sharding import PartitionSpec as P

AXES = (("x", "y", "z"), ("y", "z", "x"), ("z", "x", "y"))
MESH = pl.DeviceIdType.MESH
BF16 = jnp.bfloat16
F32 = jnp.float32
DN_T = (((1,), (1,)), ((), ()))


def dot(a, b):
    return jnp.dot(a, b, preferred_element_type=F32)


def kernel(
    hid, w, gin, rt, gt,
    mixed, ghid, gwt,
    go, ps, ra1, rb1, fl1, fr1, ra2, rb2, fl2, fr2, ra3, rb3, fl3, fr3,
    wv, hv, ht, mv, rv, acc, gws, ghr, gm, info, mst,
    ag_s, ag_r, rs_s, rs_r, w_s, w_r, h_s, h_r, in_s, in_r, gw_s, gw_r, gh_s, gh_r,
    wl, hl, gl, gwl, outl,
):
    dp = lax.axis_index("dp")
    ex = lax.axis_index("expert")
    z, y = lax.div(dp, 4), lax.rem(dp, 4)
    x, c = lax.div(ex, 2), lax.rem(ex, 2)
    oc = 1 - c
    co = {"x": x, "y": y, "z": z}
    ras, rbs, fls, frs = (ra1, ra2, ra3), (rb1, rb2, rb3), (fl1, fl2, fl3), (fr1, fr2, fr3)

    def at(axis, delta):
        return lax.rem(co[axis] + (delta + 4), 4)

    def near(axis, delta):
        q = dict(co)
        q[axis] = at(axis, delta)
        return (q["z"] * 4 + q["y"], q["x"] * 2 + c)

    partner = (dp, x * 2 + oc)

    def remote(src, dst, ssem, rsem, device):
        return pltpu.make_async_remote_copy(
            src_ref=src, dst_ref=dst, send_sem=ssem, recv_sem=rsem, device_id=device, device_id_type=MESH
        )

    row = lax.broadcasted_iota(jnp.int32, (8, 128), 0)
    eid = x * 2 + lax.rem(row, 2)
    is0 = rt[0:1, :] == eid
    is1 = rt[1:2, :] == eid
    gate = jnp.where(is0, gt[0:1, :], 0.0) + jnp.where(is1, gt[1:2, :], 0.0)
    named = jnp.where(is0, 1.0, 0.0) + jnp.where(is1, 1.0, 0.0)
    before = jnp.where(
        lax.broadcasted_iota(jnp.int32, (128, 128), 0) < lax.broadcasted_iota(jnp.int32, (128, 128), 1), 1.0, 0.0
    )
    rank = dot(jnp.concatenate([named, named], axis=0).astype(BF16), before.astype(BF16))[0:8, :]
    info[dp] = jnp.where(row < 2, jnp.where(named > 0.5, rank, -1.0), gate)

    barrier = pltpu.get_barrier_semaphore()

    def greet(k, carry):
        pl.semaphore_signal(barrier, inc=1, device_id=(lax.rem(dp + k, 16), ex), device_id_type=MESH)
        return carry

    lax.fori_loop(1, 16, greet, 0)
    for device in (near("x", 1), near("x", -1), partner):
        pl.semaphore_signal(barrier, inc=1, device_id=device, device_id_type=MESH)
    pl.semaphore_wait(barrier, 18)

    def slab(k, p, j, h):
        i1, i2 = co[AXES[p][0]], co[AXES[p][1]]
        if k == 0:
            return go.at[p, i1, i2, j, pl.ds(64 * h, 64)]
        if k == 1:
            return go.at[p, i1, j, pl.ds(2 * h, 2)]
        return go.at[p, j, pl.ds(2 * h, 2)]

    def ag_copy(k, p, n, receive):
        axis = AXES[p][2 - k]
        own, left, right, far = at(axis, 0), at(axis, -1), at(axis, 1), at(axis, 2)
        h = (0, 1, 1, 0, 0, 1)[n]
        j = ((left, right, left, right, far, far) if receive else (own, own, own, own, left, right))[n]
        dst = slab(k, p, j, h)
        src = dst
        if k == 0 and n < 4 and not receive:
            src = gin.at[pl.ds(64 * h, 64), pl.ds(256 * p, 256)]
        device = near(axis, (1, -1, 1, -1, 1, -1)[n])
        return remote(src, dst, ag_s.at[p, k, n], ag_r.at[p, k, n], device)

    def ag_start(k, p):
        for n in range(4):
            ag_copy(k, p, n, False).start()

    def ag_relay(k, p):
        for n in range(2):
            ag_copy(k, p, n, True).wait_recv()
            ag_copy(k, p, n + 4, False).start()

    def ag_finish(k, p):
        for n in range(2, 6):
            ag_copy(k, p, n, True).wait_recv()

    def chunk(k, p, j, h):
        i1, i2 = co[AXES[p][0]], co[AXES[p][1]]
        if k == 0:
            return ps.at[p, j, pl.ds(2 * h, 2)]
        if k == 1:
            return ps.at[p, i1, j, pl.ds(2 * h, 2)]
        return ps.at[p, i1, i2, j, pl.ds(64 * h, 64)]

    def half(ref, k, p, h):
        return ref.at[p, pl.ds(2 * h, 2)] if k < 2 else ref.at[p, pl.ds(64 * h, 64)]

    def rs_copy(k, p, n):
        axis = AXES[p][k]
        h = (0, 1, 1, 0, 0, 1)[n]
        j = at(axis, (2, 2, 1, -1, 1, -1)[n])
        if n == 0:
            dst = ras[k].at[p]
        elif n == 1:
            dst = rbs[k].at[p]
        else:
            dst = half((fls, frs)[n % 2][k] if n > 3 else (fls, frs)[n - 2][k], k, p, h)
        device = near(axis, (1, -1, 1, -1, 1, -1)[n])
        return remote(chunk(k, p, j, h), dst, rs_s.at[p, k, n], rs_r.at[p, k, n], device)

    def add_into(dst, sources, k):
        if k == 2:
            total = dst[...].astype(F32)
            for source in sources:
                total = total + source[...].astype(F32)
            dst[...] = total.astype(BF16)
            return
        count = dst.shape[0]
        if k == 0:
            def one(n, carry):
                a, b = lax.div(n, 4), lax.rem(n, 4)
                total = dst[a, b].astype(F32)
                for source in sources:
                    total = total + source[a, b].astype(F32)
                dst[a, b] = total.astype(BF16)
                return carry

            lax.fori_loop(0, count * 4, one, 0)
        else:
            def one(n, carry):
                total = dst[n].astype(F32)
                for source in sources:
                    total = total + source[n].astype(F32)
                dst[n] = total.astype(BF16)
                return carry

            lax.fori_loop(0, count, one, 0)

    def rs_relay(k, p):
        axis = AXES[p][k]
        rs_copy(k, p, 0).wait_recv()
        add_into(chunk(k, p, at(axis, 1), 0), (ras[k].at[p],), k)
        rs_copy(k, p, 4).start()
        rs_copy(k, p, 1).wait_recv()
        add_into(chunk(k, p, at(axis, -1), 1), (rbs[k].at[p],), k)
        rs_copy(k, p, 5).start()

    def rs_finish(k, p):
        for n in range(2, 6):
            rs_copy(k, p, n).wait_recv()
        i1, i2, i3 = (co[axis] for axis in AXES[p])
        if k == 0:
            add_into(ps.at[p, i1], (fls[k].at[p], frs[k].at[p]), k)
        elif k == 1:
            add_into(ps.at[p, i1, i2], (fls[k].at[p], frs[k].at[p]), k)
        else:
            total = ps[p, i1, i2, i3].astype(F32) + fls[k][p].astype(F32) + frs[k][p].astype(F32)
            mst[:, 256 * p:256 * (p + 1)] = total.astype(BF16)

    for p in range(3):
        ag_start(0, p)

    def info_copy(k, receive):
        place = lax.rem(dp + 16 - k, 16) if receive else dp
        return remote(info.at[dp], info.at[place], in_s.at[k], in_r.at[k], (lax.rem(dp + k, 16), ex))

    def info_start(k, carry):
        info_copy(k, False).start()
        return carry

    lax.fori_loop(1, 16, info_start, 0)

    def h_copy(e, device):
        return remote(hid, hv.at[:, pl.ds(pl.multiple_of(e * 64, 64), 64), :], h_s, h_r, device)

    def w_copy(b, e, of, device):
        cols = pl.ds(pl.multiple_of(b * 1536 + of * 768, 128), 768)
        rows = pl.ds(pl.multiple_of(e * 512, 512), 512)
        return remote(w.at[:, cols], wv.at[rows, pl.ds(b * 768, 768)], w_s.at[b], w_r.at[b], device)

    def w_local(b):
        cols = pl.ds(pl.multiple_of(b * 1536 + c * 768, 128), 768)
        rows = pl.ds(pl.multiple_of(c * 512, 512), 512)
        return pltpu.make_async_copy(w.at[:, cols], wv.at[rows, pl.ds(b * 768, 768)], wl.at[b])

    h_copy(c, partner).start()
    for b in range(4):
        w_copy(b, c, oc, partner).start()
    h_local = pltpu.make_async_copy(hid, hv.at[:, pl.ds(pl.multiple_of(c * 64, 64), 64), :], hl)
    h_local.start()

    def g_local(p):
        i1, i2, i3 = (co[axis] for axis in AXES[p])
        return pltpu.make_async_copy(gin.at[:, pl.ds(256 * p, 256)], go.at[p, i1, i2, i3], gl.at[p])

    for p in range(3):
        g_local(p).start()
    for b in range(4):
        w_local(b).start()

    for p in range(3):
        ag_relay(0, p)
    for p in range(3):
        g_local(p).wait()
        ag_finish(0, p)
        ag_start(1, p)
    for p in range(3):
        ag_relay(1, p)
    for p in range(3):
        ag_finish(1, p)
        ag_start(2, p)

    h_local.wait()
    h_copy(oc, partner).wait_recv()

    def info_wait(k, carry):
        info_copy(k, True).wait_recv()
        return carry

    lax.fori_loop(1, 16, info_wait, 0)
    slot = lax.broadcasted_iota(jnp.int32, (128, 128), 0).astype(F32)
    lane = lax.broadcasted_iota(jnp.int32, (128, 128), 1)

    def mix(d, carry):
        part = info[d]
        first = jnp.where(part[0:1, :] == slot, part[2:3, :], 0.0)
        second = jnp.where(part[1:2, :] == slot - 64.0, part[3:4, :], 0.0)
        spread = first + second
        gm[d] = spread.astype(BF16)
        turned = spread.T
        rows = hv[d]
        zz, yy = lax.div(d, 4), lax.rem(d, 4)
        mv[zz, yy, :, 0:512] = dot(jnp.where(lane < 64, turned, 0.0).astype(BF16), rows).astype(BF16)
        mv[zz, yy, :, 512:1024] = dot(jnp.where(lane < 64, 0.0, turned).astype(BF16), rows).astype(BF16)
        return carry

    lax.fori_loop(0, 16, mix, 0)

    for b in range(4):
        w_local(b).wait()
        w_copy(b, oc, c, partner).wait_recv()

    def forward(p, k):
        def tile(n, carry):
            if p == 0:
                left = mv[n]
                cols = k * 768
            elif p == 1:
                left = mv[:, k]
                cols = n * 768 + 256
            else:
                left = mv[k]
                cols = n * 768 + 512
            right = wv[:, pl.ds(pl.multiple_of(cols, 128), 256)]
            out = dot(left.reshape(512, 1024), right).astype(BF16).reshape(4, 128, 256)
            if p < 2:
                ps[p, k, :, n] = out
            else:
                ps[p, k, n] = out
            return carry

        lax.fori_loop(0, 4, tile, 0)

    for p in range(3):
        forward(p, at(AXES[p][0], 2))
        rs_copy(0, p, 0).start()
        rs_copy(0, p, 1).start()
        ag_relay(2, p)
    for p in range(3):
        forward(p, at(AXES[p][0], 1))
        rs_copy(0, p, 2).start()
        forward(p, at(AXES[p][0], -1))
        rs_copy(0, p, 3).start()
    for p in range(3):
        forward(p, at(AXES[p][0], 0))

    for e in range(2):
        def turn(n, carry, e=e):
            pair = jnp.concatenate([hv[n * 2, e * 64:e * 64 + 64, :], hv[n * 2 + 1, e * 64:e * 64 + 64, :]], axis=0)
            ht[e, :, pl.ds(pl.multiple_of(n * 128, 128), 128)] = pair.T
            return carry

        lax.fori_loop(0, 8, turn, 0)

    for p in range(3):
        ag_finish(2, p)

    def gw_out(b, mine):
        e = c if mine else oc
        cols = pl.ds(pl.multiple_of(b * 1536 + c * 768, 128), 768)
        if mine:
            return pltpu.make_async_copy(gws.at[e], gwt.at[:, cols], gwl.at[b])
        return remote(gws.at[e], gwt.at[:, cols], gw_s.at[b], gw_r.at[b], partner)

    def gw_in(b):
        cols = pl.ds(pl.multiple_of(b * 1536 + oc * 768, 128), 768)
        return remote(gws.at[c], gwt.at[:, cols], gw_s.at[b], gw_r.at[b], partner)

    def routed(b):
        def one(d, carry):
            zz, yy = lax.div(d, 4), lax.rem(d, 4)
            left = gm[d]
            start = pl.multiple_of(d * 64, 64)
            for p, right in enumerate((go[0, b, yy, zz], go[1, yy, zz, b], go[2, zz, b, yy])):
                out = dot(left, right).astype(BF16)
                rv[0, pl.ds(start, 64), 256 * p:256 * (p + 1)] = out[0:64]
                rv[1, pl.ds(start, 64), 256 * p:256 * (p + 1)] = out[64:128]
            return carry

        lax.fori_loop(0, 16, one, 0)

    def weight_grad(b, e):
        def one(n, carry):
            cols = pl.ds(pl.multiple_of(n * 256, 256), 256)
            gws[e, :, cols] = dot(ht[e], rv[e, :, cols]).astype(BF16)
            return carry

        lax.fori_loop(0, 3, one, 0)

    def hidden_grad(b, e):
        def one(n, carry):
            rows = pl.ds(pl.multiple_of(n * 256, 256), 256)
            right = wv[pl.ds(pl.multiple_of(e * 512, 512), 512), pl.ds(b * 768, 768)]
            out = lax.dot_general(rv[e, rows, :], right, DN_T, preferred_element_type=F32)
            acc[e, rows, :] = out if b == 0 else acc[e, rows, :] + out
            return carry

        lax.fori_loop(0, 4, one, 0)

    def backward(b):
        routed(b)
        if b:
            gw_out(b - 1, False).wait_send()
        weight_grad(b, oc)
        gw_out(b, False).start()
        hidden_grad(b, oc)
        if b:
            gw_out(b - 1, True).wait()
        weight_grad(b, c)
        gw_out(b, True).start()
        hidden_grad(b, c)

    backward(0)
    for p in range(3):
        rs_relay(0, p)
    backward(1)
    backward(2)
    backward(3)

    gh_copy = remote(hv.at[:, 0:64, :], ghr, gh_s, gh_r, partner)

    def pack(d, carry):
        hv[d, 0:64, :] = acc[oc, pl.ds(pl.multiple_of(d * 64, 64), 64), :].astype(BF16)
        return carry

    lax.fori_loop(0, 16, pack, 0)
    gh_copy.start()
    for p in range(3):
        rs_finish(0, p)
        for n in range(4):
            rs_copy(1, p, n).start()
    gh_copy.wait_recv()

    def close(d, carry):
        own = acc[c, pl.ds(pl.multiple_of(d * 64, 64), 64), :]
        hv[d, 64:128, :] = (own + ghr[d].astype(F32)).astype(BF16)
        return carry

    lax.fori_loop(0, 16, close, 0)
    gh_out = pltpu.make_async_copy(hv.at[:, 64:128, :], ghid, outl.at[0])
    gh_out.start()
    for p in range(3):
        rs_relay(1, p)
    for p in range(3):
        rs_finish(1, p)
        for n in range(4):
            rs_copy(2, p, n).start()
    for p in range(3):
        rs_relay(2, p)
    for p in range(3):
        rs_finish(2, p)
    mixed_out = pltpu.make_async_copy(mst, mixed, outl.at[1])
    mixed_out.start()

    for p in range(3):
        for k in range(3):
            for n in range(6):
                ag_copy(k, p, n, False).wait_send()
                rs_copy(k, p, n).wait_send()

    def info_end(k, carry):
        info_copy(k, False).wait_send()
        return carry

    lax.fori_loop(1, 16, info_end, 0)
    h_copy(c, partner).wait_send()
    for b in range(4):
        w_copy(b, c, oc, partner).wait_send()
        gw_in(b).wait_recv()
    gw_out(3, False).wait_send()
    gw_out(3, True).wait()
    gh_copy.wait_send()
    gh_out.wait()
    mixed_out.wait()


def body(hidden, down_weight, grad_out, routing, gates):
    dma = pltpu.SemaphoreType.DMA
    sums = []
    for lead, rows in (((2, 4), 128), ((2,), 128), ((), 64)):
        whole = {2: (4, 4, 128, 256), 1: (4, 128, 256), 0: (128, 256)}[len(lead)]
        sums += [pltpu.VMEM((3, *lead, rows, 256), BF16)] * 2 + [pltpu.VMEM((3, *whole), BF16)] * 2
    anywhere = pl.BlockSpec(memory_space=pl.ANY)
    inside = pl.BlockSpec(memory_space=pltpu.VMEM)
    mixed, ghid, gwt = pl.pallas_call(
        kernel,
        out_shape=(
            jax.ShapeDtypeStruct((128, 768), BF16),
            jax.ShapeDtypeStruct((16, 64, 512), BF16),
            jax.ShapeDtypeStruct((512, 6144), BF16),
        ),
        in_specs=[anywhere, anywhere, anywhere, inside, inside],
        out_specs=(anywhere, anywhere, anywhere),
        scratch_shapes=[
            pltpu.VMEM((3, 4, 4, 4, 128, 256), BF16),
            pltpu.VMEM((3, 4, 4, 4, 128, 256), BF16),
            *sums,
            pltpu.VMEM((1024, 3072), BF16),
            pltpu.VMEM((16, 128, 512), BF16),
            pltpu.VMEM((2, 512, 1024), BF16),
            pltpu.VMEM((4, 4, 128, 1024), BF16),
            pltpu.VMEM((2, 1024, 768), BF16),
            pltpu.VMEM((2, 1024, 512), F32),
            pltpu.VMEM((2, 512, 768), BF16),
            pltpu.VMEM((16, 64, 512), BF16),
            pltpu.VMEM((16, 128, 128), BF16),
            pltpu.VMEM((16, 8, 128), F32),
            pltpu.VMEM((128, 768), BF16),
            dma((3, 3, 6)), dma((3, 3, 6)), dma((3, 3, 6)), dma((3, 3, 6)),
            dma((4,)), dma((4,)), dma(()), dma(()), dma((16,)), dma((16,)),
            dma((4,)), dma((4,)), dma(()), dma(()),
            dma((4,)), dma(()), dma((3,)), dma((4,)), dma((2,)),
        ],
        compiler_params=pltpu.CompilerParams(
            collective_id=0, has_side_effects=True, vmem_limit_bytes=67043328
        ),
    )(
        hidden.reshape(16, 64, 512),
        down_weight[0],
        grad_out,
        routing.T,
        gates.T,
    )
    return mixed, ghid.reshape(1, 1024, 512), gwt[None]


def solution(mesh):
    return jax.shard_map(
        body,
        mesh=mesh,
        in_specs=(
            P("expert", None, "dp"),
            P("expert", "dp", None),
            P("dp", "expert"),
            P("dp", None),
            P("dp", None),
        ),
        out_specs=(P("dp", "expert"), P("expert", None, "dp"), P("expert", "dp", None)),
        check_vma=False,
    )
```

time: 414 us -> 145 us (0.35)
  waiting for transfers between devices: 263 us -> 0 us
  Pallas kernels: 0 us -> 131 us
  matrix products: 39.8 us -> 0 us
  local copies, waits for them, and re-layouts: 49 us -> 10.1 us
  other arithmetic: 35.1 us -> 0 us
  between operations: 14.1 us -> 0.64 us
  starting transfers between devices: 11.7 us -> 0 us
    pallas_call x0 -> x1, Pallas kernels: none -> 131 us  [body(): pl.pallas_call(kernel, out_shape=(jax.ShapeDtypeStruct((128, 768), BF16),...]
    all_to_all x2 -> x0, waiting for transfers between devices: 127 us -> none  [the longest x1 127 us: body(): lax.all_to_all(shards, 'expert', split_axis=0, concat_axis=2, tiled=True)]
    reduce_scatter x1 -> x0, waiting for transfers between devices: 93.8 us -> none  [body(): lax.psum_scatter(jnp.dot(hidden_rows, weight, preferred_element_type=jnp....]
    all_gather x1 -> x0, waiting for transfers between devices: 41.9 us -> none  [body(): shards = lax.all_gather(routed, 'dp', axis=1, tiled=True)]
    dot_general x5 -> x0, matrix products: 39.8 us -> none  [the longest x1 13.1 us: body(): lax.dot_general(hidden_rows, grad_rows, (((0,), (0,)), ((), ())), preferr...]
    unnamed x1 -> x0, other arithmetic: 34.3 us -> none
    all_gather x1 -> x0, local copies, waits for them, and re-layouts: 16.5 us -> none  [body(): shards = lax.all_gather(routed, 'dp', axis=1, tiled=True)]
    all_to_all x2 -> x0, starting transfers between devices: 11.6 us -> none  [the longest x1 6.24 us: body(): lax.all_to_all(shards, 'expert', split_axis=0, concat_axis=2, tiled=True)]
  transfers between devices with their start and end apart: 4 -> 0, of which waited for: 3 -> 0; matrix products, arithmetic and copies ran while one was open for 18% -> 0% of each run, Pallas kernels for 0% -> 0%
where the time goes in v1:
time: 145 us; the launch traced here: 142 us
  Pallas kernels  131 us (90%)
  local copies, waits for them, and re-layouts  10.1 us (7%)
    pallas_call x1, Pallas kernels, body(): pl.pallas_call(kernel, out_shape=(jax.ShapeDtypeStruct((128, 768), BF16),...  131 us
    unnamed x3, local copies, waits for them, and re-layouts  10.1 us

profile of v1, /device:TPU:1, one launch (start us, length us, event | category | flops | bytes accessed | tf_op | source)
XLA Modules:
  0.0 142.1 jit_solution(3503130081760670018)
XLA Ops:
  0.6 131.4 %shard_map.76 = (bf16[128,768]{1,0:T(8,128)(2,1)}, bf16[16,64,512]{2,1,0:T(8,128)(2,1)}, bf16[512,6144]{1,0:T(8,128)(2,1)}) custom-call(bf16[16,64,512]{2,1,0:T(8,128)(2,1)} %bitcast.9, bf16[512,6144]{1,0:T(8,128)(2,1)} %bitcast.7, bf16[128,768]{1,0:T(8,128)(2,1)} %gin.1, s32[2,128]{1,0:T(2,128)} %bitcast.10, f32[2,128]{1,0:T(2,128)} %bitcast.11), custom_call_target="tpu_custom_call" | custom-call | tf_op jit(solution)/shard_map/pallas_call | solution.py:434
  132.0 1.6 %copy.11 = bf16[128,768]{1,0:T(8,128)(2,1)} copy(bf16[128,768]{1,0:T(8,128)(2,1)} %get-tuple-element.12) | data formatting | bytes 393216
  133.6 2.3 %copy.12 = bf16[1,1024,512]{2,1,0:T(8,128)(2,1)} copy(bf16[1,1024,512]{2,1,0:T(8,128)(2,1)} %bitcast.8) | data formatting | bytes 2097152
  135.9 6.2 %copy.13 = bf16[1,512,6144]{2,1,0:T(8,128)(2,1)} copy(bf16[1,512,6144]{2,1,0:T(8,128)(2,1)} %bitcast.6) | data formatting | bytes 12582912

commit v2 on v0

v2 whole, which is shorter than its diff:
```python
import jax
import jax.numpy as jnp
from jax import lax
from jax.experimental import pallas as pl
from jax.experimental.pallas import tpu as pltpu
from jax.sharding import PartitionSpec as P

AXES = (("x", "y", "z"), ("y", "z", "x"), ("z", "x", "y"))
MESH = pl.DeviceIdType.MESH
BF16 = jnp.bfloat16
F32 = jnp.float32
RATE = 1.4
HOP = 2.0
DN_T = (((1,), (1,)), ((), ()))


def dot(a, b):
    return jnp.dot(a, b, preferred_element_type=F32)


class Clock:
    def __init__(self):
        self.now, self.links, self.pending, self.done, self.count = 0.0, {}, [], set(), 0

    def send(self, copy, size, link):
        copy.start()
        begin = max(self.now, self.links.get(link, 0.0))
        self.links[link] = begin + size / RATE
        return self.links[link] + HOP

    def later(self, ready, needs, act):
        self.count += 1
        self.pending.append((ready, self.count, needs, act))

    def step(self, limit):
        able = [item for item in self.pending if item[0] <= limit and self.done.issuperset(item[2])]
        if not able:
            return False
        item = min(able, key=lambda item: item[:2])
        self.pending.remove(item)
        self.now = max(self.now, item[0])
        item[3]()
        return True

    def flush(self):
        while self.step(self.now):
            pass

    def wait(self, tags):
        while not self.done.issuperset(tags):
            assert self.step(float("inf"))

    def run(self, cost, act, *args):
        self.flush()
        act(*args)
        self.now += cost


def kernel(
    hid, w, gin, rt, gt,
    mixed, ghid, gwt,
    go, ps, ra1, rb1, fl1, fr1, ra2, rb2, fl2, fr2, ra3, rb3, fl3, fr3,
    wv, hv, ht, mv, rv, acc, gws, ghr, gm, info, mst,
    ag_s, ag_r, rs_s, rs_r, w_s, w_r, h_s, h_r, in_s, in_r, gw_s, gw_r, gh_s, gh_r,
    wl, hl, gl, gwl, outl,
):
    dp = lax.axis_index("dp")
    ex = lax.axis_index("expert")
    z, y = lax.div(dp, 4), lax.rem(dp, 4)
    x, c = lax.div(ex, 2), lax.rem(ex, 2)
    oc = 1 - c
    co = {"x": x, "y": y, "z": z}
    clock = Clock()

    def at(axis, delta):
        return lax.rem(co[axis] + delta, 4)

    def rel(axis, place):
        return lax.rem(place + 4 - co[axis], 4)

    def near(axis, delta):
        q = dict(co)
        q[axis] = at(axis, delta % 4)
        return (q["z"] * 4 + q["y"], q["x"] * 2 + c)

    partner = (dp, x * 2 + oc)

    def remote(src, dst, ssem, rsem, device):
        return pltpu.make_async_remote_copy(
            src_ref=src, dst_ref=dst, send_sem=ssem, recv_sem=rsem, device_id=device, device_id_type=MESH
        )

    barrier = pltpu.get_barrier_semaphore()

    for device in [near(axis, side) for axis in "xyz" for side in (1, -1)] + [near("y", 2), near("z", 2), partner]:
        pl.semaphore_signal(barrier, inc=1, device_id=device, device_id_type=MESH)

    row = lax.broadcasted_iota(jnp.int32, (8, 128), 0)
    eid = x * 2 + lax.rem(row, 2)
    is0 = rt[0:1, :] == eid
    is1 = rt[1:2, :] == eid
    gate = jnp.where(is0, gt[0:1, :], 0.0) + jnp.where(is1, gt[1:2, :], 0.0)
    named = jnp.where(is0, 1.0, 0.0) + jnp.where(is1, 1.0, 0.0)
    before = jnp.where(
        lax.broadcasted_iota(jnp.int32, (128, 128), 0) < lax.broadcasted_iota(jnp.int32, (128, 128), 1), 1.0, 0.0
    )
    rank = dot(jnp.concatenate([named, named], axis=0).astype(BF16), before.astype(BF16))[0:8, :]
    info[0, 0] = jnp.where(row < 2, jnp.where(named > 0.5, rank, -1.0), gate)

    def w_local(b):
        cols = pl.ds(pl.multiple_of(b * 1536 + c * 768, 128), 768)
        rows = pl.ds(pl.multiple_of(c * 512, 512), 512)
        return pltpu.make_async_copy(w.at[:, cols], wv.at[rows, pl.ds(b * 768, 768)], wl)

    def g_local(p, h):
        return pltpu.make_async_copy(
            gin.at[pl.ds(64 * h, 64), pl.ds(256 * p, 256)], go.at[p, h, 0, 0, 0], gl
        )

    h_local = pltpu.make_async_copy(hid, hv.at[:, pl.ds(pl.multiple_of(c * 64, 64), 64), :], hl)
    h_local.start()
    for p in range(3):
        for h in range(2):
            g_local(p, h).start()
    for b in range(4):
        w_local(b).start()
    pl.semaphore_wait(barrier, 9)

    def region(ref, p, h, k, g, q):
        one, rest = pl.ds(0, 1), pl.ds(1, 3)
        if k == 2:
            return ref.at[p, h, 0, 0, pl.ds(q, 1) if isinstance(q, int) else q]
        if k == 1:
            return ref.at[p, h, 0, q, rest if g & 1 else one]
        return ref.at[p, h, q, rest if g & 2 else one, rest if g & 1 else one]

    BLOCKS = (1, 3, 3, 9)
    SIDES = (1, -1, 1, -1, 1, -1)
    HALVES = (0, 1, 1, 0, 0, 1)

    def slot(k, g):
        return (0, 4, 6)[k] + g

    def ag_copy(k, p, g, n):
        axis, h = AXES[p][k], HALVES[n]
        q = (3, 1, 3, 1, 2, 2)[n]
        dst = region(go, p, h, k, g, q)
        src = region(go, p, h, k, g, (0, 0, 0, 0, 3, 1)[n])
        s = slot(k, g)
        return remote(src, dst, ag_s.at[k], ag_r.at[p, s, min(n // 2, 1)], near(axis, SIDES[n]))

    def ag_send(k, p, g, n):
        return clock.send(ag_copy(k, p, g, n), BLOCKS[g], (AXES[p][k], SIDES[n]))

    def taken(ref, k, p, g, late):
        some = region(go, p, pl.ds(0, 2), k, g, pl.ds(1, 2) if late else pl.ds(1, 1))
        remote(some, some, ref, ref, partner).wait_recv()

    def ag_start(k, p, g):
        due = [ag_send(k, p, g, n) for n in range(4)]

        def relay():
            taken(ag_r.at[p, slot(k, g), 0], k, p, g, False)
            last = [ag_send(k, p, g, n) for n in (4, 5)]
            clock.done.add(("passed", k, p, g))
            clock.later(max(due + last), (), finish)

        def finish():
            taken(ag_r.at[p, slot(k, g), 1], k, p, g, True)
            clock.done.add(("ag", k, p, g))
            if (k, g) == (2, 0):
                ag_start(1, p, 1)
                ag_start(0, p, 1)
            elif k == 1:
                ag_start(0, p, 2 + g)

        clock.later(max(due[:2]), (), relay)

    def rs_place(k, p, g, n):
        one, rest = pl.ds(0, 1), pl.ds(1, 3)
        a, b = (rest if g & 2 else one), (rest if g & 1 else one)
        if n < 2:
            ref = ((ra1, ra2, ra3), (rb1, rb2, rb3))[n][k].at[p]
        else:
            ref = ((fl1, fl2, fl3), (fr1, fr2, fr3))[n % 2][k].at[p, HALVES[n]]
        return ref.at[a, b] if k == 0 else ref.at[b] if k == 1 else ref

    def rs_copy(k, p, g, n):
        src = region(ps, p, HALVES[n], k, g, (2, 2, 1, 3, 1, 3)[n])
        s = slot(k, g)
        return remote(src, rs_place(k, p, g, n), rs_s.at[k], rs_r.at[p, s, min(n // 2, 1)], near(AXES[p][k], SIDES[n]))

    def rs_send(k, p, g, n):
        return clock.send(rs_copy(k, p, g, n), BLOCKS[g], (AXES[p][k], SIDES[n]))

    def add_into(k, g, dst, sources):
        def total(*index):
            out = dst[index].astype(F32)
            for source in sources:
                out = out + source[index].astype(F32)
            dst[index] = out.astype(BF16)

        if k > 0:
            for b in range(3 if g & 1 else 1):
                total(b)
        else:
            wide = 3 if g & 1 else 1

            def one(n, carry):
                total(lax.div(n, wide), lax.rem(n, wide))
                return carry

            lax.fori_loop(0, BLOCKS[g], one, 0)
        clock.now += 0.03 * BLOCKS[g]

    def rs_start(k, p, g):
        due = [rs_send(k, p, g, n) for n in range(4)]

        def relay():
            taken(rs_r.at[p, slot(k, g), 0], k, p, g, False)
            last = []
            for n in range(2):
                add_into(k, g, region(ps, p, n, k, g, (1, 3)[n]), (rs_place(k, p, g, n),))
                last.append(rs_send(k, p, g, n + 4))
            clock.later(max(due + last), (("fwd", p, 0),), finish)
            if k == 0:
                for follower in {3: (2, 1), 2: (0,)}.get(g, ()):
                    rs_start(0, p, follower)

        def finish():
            taken(rs_r.at[p, slot(k, g), 1], k, p, g, True)
            for h in range(2):
                places = [rs_place(k, p, g, m) for m in range(2, 6) if HALVES[m] == h]
                add_into(k, g, region(ps, p, h, k, g, 0), places)
            done = clock.done
            done.add(("rs", k, p, g))
            if k == 0 and g & 2:
                rs_start(1, p, g & 1)
            if (k, g) in ((0, 1), (1, 1)) and done.issuperset((("rs", 0, p, 1), ("rs", 1, p, 1))):
                rs_start(2, p, 0)
            if done.issuperset(("rs", m, p, 0) for m in range(3)):
                for h in range(2):
                    mst[64 * h:64 * h + 64, 256 * p:256 * (p + 1)] = ps[p, h, 0, 0, 0]
                done.add(("sum", p))

        clock.later(max(due[:2]), (), relay)

    own = go.at[:, :, 0, 0, 0]
    pltpu.make_async_copy(own, own, gl).wait()
    def info_copy(axis, n):
        q, side = ((3, 1), (1, -1), (2, 2))[n]
        src, dst = (info.at[0, 0], info.at[0, q]) if axis == "y" else (info.at[0], info.at[q])
        i = ("y", "z").index(axis) * 3 + n
        return remote(src, dst, in_s.at[i], in_r.at[i], near(axis, side))

    def info_start(axis):
        due = [clock.send(info_copy(axis, n), 0.1, (axis, (1, -1, 1)[n])) for n in range(3)]

        def finish():
            for n in range(3):
                info_copy(axis, n).wait_recv()
            clock.done.add(("info", axis))
            if axis == "y":
                info_start("z")

        clock.later(max(due) + 1.0, (), finish)

    info_start("y")
    for k in (2, 1, 0):
        for p in range(3):
            ag_start(k, p, 0)

    def h_copy(e, device):
        return remote(hid, hv.at[:, pl.ds(pl.multiple_of(e * 64, 64), 64), :], h_s, h_r, device)

    def w_copy(b, e, of, device):
        cols = pl.ds(pl.multiple_of(b * 1536 + of * 768, 128), 768)
        rows = pl.ds(pl.multiple_of(e * 512, 512), 512)
        return remote(w.at[:, cols], wv.at[rows, pl.ds(b * 768, 768)], w_s, w_r, device)

    h_copy(c, partner).start()
    for b in range(4):
        w_copy(b, c, oc, partner).start()

    def turning(e):
        def turn(n, carry):
            pair = jnp.concatenate([hv[n * 2, e * 64:e * 64 + 64, :], hv[n * 2 + 1, e * 64:e * 64 + 64, :]], axis=0)
            ht[e, :, pl.ds(pl.multiple_of(n * 128, 128), 128)] = pair.T
            return carry

        lax.fori_loop(0, 8, turn, 0)

    place = lax.broadcasted_iota(jnp.int32, (128, 128), 0).astype(F32)
    lane = lax.broadcasted_iota(jnp.int32, (128, 128), 1)

    def mix(d, carry):
        zz, yy = lax.div(d, 4), lax.rem(d, 4)
        part = info[rel("z", zz), rel("y", yy)]
        first = jnp.where(part[0:1, :] == place, part[2:3, :], 0.0)
        second = jnp.where(part[1:2, :] == place - 64.0, part[3:4, :], 0.0)
        spread = first + second
        gm[d] = spread.astype(BF16)
        turned = spread.T
        rows = hv[d]
        mv[zz, yy, :, 0:512] = dot(jnp.where(lane < 64, turned, 0.0).astype(BF16), rows).astype(BF16)
        mv[zz, yy, :, 512:1024] = dot(jnp.where(lane < 64, 0.0, turned).astype(BF16), rows).astype(BF16)
        return carry

    def mixing(m):
        lax.fori_loop(4 * m, 4 * m + 4, mix, 0)

    def forward(p, j):
        chunk_at = at(AXES[p][0], j)

        def tile(n, carry):
            if p == 0:
                left = mv[at("z", n)]
                cols = chunk_at * 768
            elif p == 1:
                left = mv[:, chunk_at]
                cols = n * 768 + 256
            else:
                left = mv[chunk_at]
                cols = n * 768 + 512
            right = wv[:, pl.ds(pl.multiple_of(cols, 128), 256)]
            out = dot(left.reshape(512, 1024), right).astype(BF16)
            for q in range(4):
                for h in range(2):
                    piece = out[128 * q + 64 * h:128 * q + 64 * h + 64]
                    if p == 0:
                        ps[p, h, j, rel("y", q), n] = piece
                    elif p == 1:
                        ps[p, h, j, rel("z", q), rel("x", n)] = piece
                    else:
                        ps[p, h, j, rel("x", n), rel("y", q)] = piece
            return carry

        lax.fori_loop(0, 4, tile, 0)
        clock.done.add(("fwd", p, j))

    def gw_out(b, mine):
        e = c if mine else oc
        cols = pl.ds(pl.multiple_of(b * 1536 + c * 768, 128), 768)
        if mine:
            return pltpu.make_async_copy(gws.at[e], gwt.at[:, cols], gwl)
        return remote(gws.at[e], gwt.at[:, cols], gw_s, gw_r, partner)

    def routed(b):
        def one(d, carry):
            zz, yy = lax.div(d, 4), lax.rem(d, 4)
            left = gm[d]
            start = pl.multiple_of(d * 64, 64)
            rx, ry, rz = rel("x", b), rel("y", yy), rel("z", zz)
            for p, (i, j, k) in enumerate(((rx, ry, rz), (ry, rz, rx), (rz, rx, ry))):
                right = jnp.concatenate([go[p, 0, i, j, k], go[p, 1, i, j, k]], axis=0)
                out = dot(left, right).astype(BF16)
                rv[0, pl.ds(start, 64), 256 * p:256 * (p + 1)] = out[0:64]
                rv[1, pl.ds(start, 64), 256 * p:256 * (p + 1)] = out[64:128]
            return carry

        lax.fori_loop(0, 16, one, 0)

    def weight_grad(b, mine):
        e = c if mine else oc
        if b:
            if mine:
                gw_out(b - 1, True).wait()
            else:
                gw_out(b - 1, False).wait_send()

        def one(n, carry):
            cols = pl.ds(pl.multiple_of(n * 256, 256), 256)
            gws[e, :, cols] = dot(ht[e], rv[e, :, cols]).astype(BF16)
            return carry

        lax.fori_loop(0, 3, one, 0)
        gw_out(b, mine).start()

    def hidden_grad(b, e):
        def one(n, carry):
            rows = pl.ds(pl.multiple_of(n * 256, 256), 256)
            right = wv[pl.ds(pl.multiple_of(e * 512, 512), 512), pl.ds(b * 768, 768)]
            out = lax.dot_general(rv[e, rows, :], right, DN_T, preferred_element_type=F32)
            acc[e, rows, :] = out if b == 0 else acc[e, rows, :] + out
            return carry

        lax.fori_loop(0, 4, one, 0)

    h_local.wait()
    h_copy(oc, partner).wait_recv()
    clock.now += 4.0
    clock.run(1.0, turning, 0)
    clock.run(1.0, turning, 1)
    clock.wait([("info", "z")])
    for m in range(4):
        clock.run(0.8, mixing, m)
    mine, theirs = (wv.at[pl.ds(pl.multiple_of(e * 512, 512), 512)] for e in (c, oc))
    pltpu.make_async_copy(mine, mine, wl).wait()
    remote(theirs, theirs, w_s, w_r, partner).wait_recv()
    for j in (2, 1, 3):
        for p in range(3):
            clock.run(2.2, forward, p, j)
    for p in range(3):
        clock.later(clock.now, [("passed", 0, p, g) for g in range(4)], lambda p=p: rs_start(0, p, 3))
    for p in range(3):
        clock.run(2.2, forward, p, 0)
    clock.wait([("ag", 0, p, g) for p in range(3) for g in range(4)])
    for b in range(4):
        clock.run(2.6, routed, b)
        clock.run(1.8, weight_grad, b, False)
        clock.run(1.8, hidden_grad, b, oc)
        clock.run(1.8, weight_grad, b, True)
        clock.run(1.8, hidden_grad, b, c)

    gh_copy = remote(hv.at[:, 0:64, :], ghr, gh_s, gh_r, partner)

    def pack(d, carry):
        hv[d, 0:64, :] = acc[oc, pl.ds(pl.multiple_of(d * 64, 64), 64), :].astype(BF16)
        return carry

    def close(d, carry):
        own = acc[c, pl.ds(pl.multiple_of(d * 64, 64), 64), :]
        hv[d, 64:128, :] = (own + ghr[d].astype(F32)).astype(BF16)
        return carry

    clock.run(0.5, lax.fori_loop, 0, 16, pack, 0)
    gh_copy.start()
    clock.run(4.0, lambda: None)
    clock.flush()
    gh_copy.wait_recv()
    clock.run(0.5, lax.fori_loop, 0, 16, close, 0)
    gh_out = pltpu.make_async_copy(hv.at[:, 64:128, :], ghid, outl.at[0])
    gh_out.start()
    clock.wait([("sum", p) for p in range(3)])
    mixed_out = pltpu.make_async_copy(mst, mixed, outl.at[1])
    mixed_out.start()

    for k, all_sent in enumerate((go.at[:, :, 0:3], go.at[:, :, 0, 0:3], go.at[:, :, 0, 0, 0:3])):
        for sem in (ag_s.at[k], rs_s.at[k]):
            remote(all_sent, all_sent, sem, sem, partner).wait_send()
    for axis in "yz":
        for n in range(3):
            info_copy(axis, n).wait_send()
    h_copy(c, partner).wait_send()
    remote(mine, mine, w_s, w_r, partner).wait_send()
    landed = gwt.at[:, 0:3072]
    remote(landed, landed, gw_s, gw_r, partner).wait_recv()
    gw_out(3, False).wait_send()
    gw_out(3, True).wait()
    gh_copy.wait_send()
    gh_out.wait()
    mixed_out.wait()


def hand_on(a, b, c, a_out, b_out, c_out, av, bv, cv, isem, osem):
    steps = [(a, av, a_out, None), (b, bv, b_out, None)] + [(c, cv, c_out, n) for n in range(8)]
    copies = []
    for i, (src, mid, dst, n) in enumerate(steps):
        if n is not None:
            rows = pl.ds(64 * n, 64)
            src, mid, dst = src.at[rows], mid.at[rows], dst.at[rows]
        copies.append(
            (pltpu.make_async_copy(src, mid, isem.at[i]), pltpu.make_async_copy(mid, dst, osem.at[i]))
        )
    for first, _ in copies:
        first.start()
    for first, second in copies:
        first.wait()
        second.start()
    for _, second in copies:
        second.wait()


def body(hidden, down_weight, grad_out, routing, gates):
    dma = pltpu.SemaphoreType.DMA
    sums = []
    for lead in ((4, 4), (4,), ()):
        sums += [pltpu.VMEM((3, *(lead or (1,)), 64, 256), BF16)] * 2
        sums += [pltpu.VMEM((3, 2, *(lead or (1,)), 64, 256), BF16)] * 2
    anywhere = pl.BlockSpec(memory_space=pl.ANY)
    inside = pl.BlockSpec(memory_space=pltpu.VMEM)
    outs = (
        jax.ShapeDtypeStruct((128, 768), BF16),
        jax.ShapeDtypeStruct((16, 64, 512), BF16),
        jax.ShapeDtypeStruct((512, 6144), BF16),
    )
    results = pl.pallas_call(
        kernel,
        out_shape=outs,
        in_specs=[anywhere, anywhere, anywhere, inside, inside],
        out_specs=(anywhere, anywhere, anywhere),
        scratch_shapes=[
            pltpu.VMEM((3, 2, 4, 4, 4, 64, 256), BF16),
            pltpu.VMEM((3, 2, 4, 4, 4, 64, 256), BF16),
            *sums,
            pltpu.VMEM((1024, 3072), BF16),
            pltpu.VMEM((16, 128, 512), BF16),
            pltpu.VMEM((2, 512, 1024), BF16),
            pltpu.VMEM((4, 4, 128, 1024), BF16),
            pltpu.VMEM((2, 1024, 768), BF16),
            pltpu.VMEM((2, 1024, 512), F32),
            pltpu.VMEM((2, 512, 768), BF16),
            pltpu.VMEM((16, 64, 512), BF16),
            pltpu.VMEM((16, 128, 128), BF16),
            pltpu.VMEM((4, 4, 8, 128), F32),
            pltpu.VMEM((128, 768), BF16),
            dma((3,)), dma((3, 7, 2)), dma((3,)), dma((3, 7, 2)),
            dma(()), dma(()), dma(()), dma(()), dma((6,)), dma((6,)),
            dma(()), dma(()), dma(()), dma(()),
            dma(()), dma(()), dma(()), dma(()), dma((2,)),
        ],
        compiler_params=pltpu.CompilerParams(
            collective_id=0, has_side_effects=True, vmem_limit_bytes=67043328
        ),
    )(
        hidden.reshape(16, 64, 512),
        down_weight[0],
        grad_out,
        routing.T,
        gates.T,
    )
    mixed, ghid, gwt = pl.pallas_call(
        hand_on,
        out_shape=outs,
        in_specs=[anywhere] * 3,
        out_specs=(anywhere,) * 3,
        scratch_shapes=[pltpu.VMEM(out.shape, BF16) for out in outs] + [dma((10,)), dma((10,))],
        compiler_params=pltpu.CompilerParams(vmem_limit_bytes=67043328),
    )(*results)
    return mixed, ghid.reshape(1, 1024, 512), gwt[None]


def solution(mesh):
    return jax.shard_map(
        body,
        mesh=mesh,
        in_specs=(
            P("expert", None, "dp"),
            P("expert", "dp", None),
            P("dp", "expert"),
            P("dp", None),
            P("dp", None),
        ),
        out_specs=(P("dp", "expert"), P("expert", None, "dp"), P("expert", "dp", None)),
        check_vma=False,
    )
```

time: 414 us -> 116 us (0.28)
  waiting for transfers between devices: 263 us -> 0 us
  Pallas kernels: 0 us -> 115 us
  local copies, waits for them, and re-layouts: 49 us -> 0 us
  matrix products: 39.8 us -> 0 us
  other arithmetic: 35.1 us -> 0 us
  between operations: 14.1 us -> 0.64 us
  starting transfers between devices: 11.7 us -> 0 us
    all_to_all x2 -> x0, waiting for transfers between devices: 127 us -> none  [the longest x1 127 us: body(): lax.all_to_all(shards, 'expert', split_axis=0, concat_axis=2, tiled=True)]
    pallas_call x0 -> x2, Pallas kernels: none -> 115 us  [the longest x1 109 us: body(): pl.pallas_call(kernel, out_shape=outs, in_specs=[anywhere, anywhere, anyw...]
    reduce_scatter x1 -> x0, waiting for transfers between devices: 93.8 us -> none  [body(): lax.psum_scatter(jnp.dot(hidden_rows, weight, preferred_element_type=jnp....]
    all_gather x1 -> x0, waiting for transfers between devices: 41.9 us -> none  [body(): shards = lax.all_gather(routed, 'dp', axis=1, tiled=True)]
    dot_general x5 -> x0, matrix products: 39.8 us -> none  [the longest x1 13.1 us: body(): lax.dot_general(hidden_rows, grad_rows, (((0,), (0,)), ((), ())), preferr...]
    unnamed x1 -> x0, other arithmetic: 34.3 us -> none
    unnamed x14 -> x0, local copies, waits for them, and re-layouts: 17 us -> none
    all_gather x1 -> x0, local copies, waits for them, and re-layouts: 16.5 us -> none  [body(): shards = lax.all_gather(routed, 'dp', axis=1, tiled=True)]
  transfers between devices with their start and end apart: 4 -> 0, of which waited for: 3 -> 0; matrix products, arithmetic and copies ran while one was open for 18% -> 0% of each run, Pallas kernels for 0% -> 0%
where the time goes in v2:
time: 116 us; the launch traced here: 115 us
  Pallas kernels  115 us (99%)
    pallas_call x1, Pallas kernels, body(): pl.pallas_call(kernel, out_shape=outs, in_specs=[anywhere, anywhere, anyw...  109 us
    pallas_call x1, Pallas kernels, body(): pl.pallas_call(hand_on, out_shape=outs, in_specs=[anywhere] * 3, out_spec...  6.11 us

profile of v2, /device:TPU:1, one launch (start us, length us, event | category | flops | bytes accessed | tf_op | source)
XLA Modules:
  0.0 115.4 jit_solution(16344140583067931170)
XLA Ops:
  0.6 108.6 %shard_map.76 = (bf16[128,768]{1,0:T(8,128)(2,1)}, bf16[16,64,512]{2,1,0:T(8,128)(2,1)}, bf16[512,6144]{1,0:T(8,128)(2,1)}) custom-call(bf16[16,64,512]{2,1,0:T(8,128)(2,1)} %bitcast.7, bf16[512,6144]{1,0:T(8,128)(2,1)} %bitcast.6, bf16[128,768]{1,0:T(8,128)(2,1)} %gin.1, s32[2,128]{1,0:T(2,128)} %bitcast.8, f32[2,128]{1,0:T(2,128)} %bitcast.9), custom_call_target="tpu_custom_call" | custom-call | tf_op jit(solution)/shard_map/pallas_call | solution.py:487
  109.3 6.1 %shard_map.77 = (bf16[128,768]{1,0:T(8,128)(2,1)}, bf16[16,64,512]{2,1,0:T(8,128)(2,1)}, bf16[512,6144]{1,0:T(8,128)(2,1)}) custom-call(bf16[128,768]{1,0:T(8,128)(2,1)} %get-tuple-element.9.a, bf16[16,64,512]{2,1,0:T(8,128)(2,1)} %get-tuple-element.10.b, bf16[512,6144]{1,0:T(8,128)(2,1)} %get-tuple-element.11.c), custom_call_target="tpu_custom_call" | custom-call | tf_op jit(solution)/shard_map/pallas_call | solution.py:522

commit v3 on v2

v3 whole, which is shorter than its diff:
```python
import jax
import jax.numpy as jnp
from jax import lax
from jax.experimental import pallas as pl
from jax.experimental.pallas import tpu as pltpu
from jax.sharding import PartitionSpec as P

AXES = (("x", "y", "z"), ("y", "z", "x"), ("z", "x", "y"))
MESH = pl.DeviceIdType.MESH
BF16 = jnp.bfloat16
F32 = jnp.float32
RATE = 1.4
HOP = 2.0
FWD, ROUTED, WEIGHT, HIDDEN = 1.1, 1.3, 0.6, 0.9
DN_T = (((1,), (1,)), ((), ()))


def dot(a, b):
    return jnp.dot(a, b, preferred_element_type=F32)


class Clock:
    def __init__(self):
        self.now, self.links, self.pending, self.done, self.count = 0.0, {}, [], set(), 0
        self.places, self.place = {}, None

    def act(self, what):
        self.places.setdefault(self.place, []).append(what)

    def send(self, copy, size, link):
        self.act(lambda: copy().start())
        begin = max(self.now, self.links.get(link, 0.0))
        self.links[link] = begin + size / RATE
        return self.links[link] + HOP

    def later(self, ready, needs, event):
        self.count += 1
        self.pending.append((ready, self.count, needs, event))

    def step(self, limit):
        able = [item for item in self.pending if item[0] <= limit and self.done.issuperset(item[2])]
        if not able:
            return False
        item = min(able, key=lambda item: item[:2])
        self.pending.remove(item)
        self.now = max(self.now, item[0])
        item[3]()
        return True

    def run(self, place, cost=0.0, tags=()):
        self.place = place
        while self.step(self.now):
            pass
        while not self.done.issuperset(tags):
            assert self.step(float("inf"))
        self.now += cost

    def emit(self, *places, index=None):
        for value, place in enumerate(places):
            todo = self.places.pop(place, ())

            def all_of(todo=todo):
                for what in todo:
                    what()

            if todo and index is not None:
                pl.when(index == value)(all_of)
            elif todo:
                all_of()


def kernel(
    hid, w, gin, rt, gt,
    mixed, ghid, gwt,
    go, ps, rx1, fl1, fr1, rx2, fl2, fr2, rx3, fl3, fr3,
    wv, hv, ht, mv, rv, acc, gws, ghr, gm, info, mst, rv_i, rv_g,
    ag_s, ag_r, rs_s, rs_r, w_s, w_r, h_s, h_r, in_s, in_r, gw_s, gw_r, gh_s, gh_r,
    wl, hl, gl, gwl, outl, rl,
):
    dp = lax.axis_index("dp")
    ex = lax.axis_index("expert")
    z, y = lax.div(dp, 4), lax.rem(dp, 4)
    x, c = lax.div(ex, 2), lax.rem(ex, 2)
    oc = 1 - c
    co = {"x": x, "y": y, "z": z}
    clock = Clock()

    def at(axis, delta):
        return lax.rem(co[axis] + delta, 4)

    def rel(axis, place):
        return lax.rem(place + 4 - co[axis], 4)

    def near(axis, delta):
        q = dict(co)
        q[axis] = at(axis, delta % 4)
        return (q["z"] * 4 + q["y"], q["x"] * 2 + c)

    partner = (dp, x * 2 + oc)

    def remote(src, dst, ssem, rsem, device):
        return pltpu.make_async_remote_copy(
            src_ref=src, dst_ref=dst, send_sem=ssem, recv_sem=rsem, device_id=device, device_id_type=MESH
        )

    barrier = pltpu.get_barrier_semaphore()

    for device in [near(axis, side) for axis in "xyz" for side in (1, -1)] + [near("y", 2), near("z", 2), partner]:
        pl.semaphore_signal(barrier, inc=1, device_id=device, device_id_type=MESH)

    def w_local(b):
        cols = pl.ds(pl.multiple_of(b * 1536 + c * 768, 128), 768)
        rows = pl.ds(pl.multiple_of(c * 512, 512), 512)
        return pltpu.make_async_copy(w.at[:, cols], wv.at[rows, pl.ds(b * 768, 768)], wl)

    def g_local(p, h):
        return pltpu.make_async_copy(
            gin.at[pl.ds(64 * h, 64), pl.ds(256 * p, 256)], go.at[p, h, 0, 0, 0], gl
        )

    h_local = pltpu.make_async_copy(hid, hv.at[:, pl.ds(pl.multiple_of(c * 64, 64), 64), :], hl)
    rt_local = pltpu.make_async_copy(rt, rv_i, rl.at[0])
    gt_local = pltpu.make_async_copy(gt, rv_g, rl.at[1])
    rt_local.start()
    gt_local.start()
    for p in range(3):
        for h in range(2):
            g_local(p, h).start()
    h_local.start()
    for b in range(4):
        w_local(b).start()
    pl.semaphore_wait(barrier, 9)

    def region(ref, p, h, k, g, q):
        one, rest = pl.ds(0, 1), pl.ds(1, 3)
        if k == 2:
            return ref.at[p, h, 0, 0, pl.ds(q, 1) if isinstance(q, int) else q]
        if k == 1:
            return ref.at[p, h, 0, q, rest if g & 1 else one]
        return ref.at[p, h, q, rest if g & 2 else one, rest if g & 1 else one]

    BLOCKS = (1, 3, 3, 9)
    BOTH = pl.ds(0, 2)

    def slot(k, g):
        return (0, 4, 6)[k] + g

    def legs(k, g, way):
        if g:
            return (0, 1, 0), (1, -1, 0), (1, 1, 1), (0, -1, 1), (0, 1, 2), (1, -1, 2)
        side = way if (k, g) in ((0, 1), (1, 0), (2, 0)) else -way
        return (BOTH, side, 0), (BOTH, -side, 1), (BOTH, side, 2)

    def size(g, leg):
        return BLOCKS[g] * (2 if leg[0] is BOTH else 1)

    def taken(ref, k, p, g, late):
        some = region(go, p, BOTH, k, g, pl.ds(1, 2) if late else pl.ds(1, 1))
        remote(some, some, ref, ref, partner).wait_recv()

    def ag_send(k, p, g, leg):
        h, side, stage = leg
        axis, came = AXES[p][k], -side % 4

        def copy():
            src = region(go, p, h, k, g, came if stage == 2 else 0)
            dst = region(go, p, h, k, g, 2 if stage == 2 else came)
            return remote(src, dst, ag_s.at[k], ag_r.at[p, slot(k, g), min(stage, 1)], near(axis, side))

        return clock.send(copy, size(g, leg), (axis, side))

    def ag_start(k, p, g):
        group = legs(k, g, 1)
        due = [(ag_send(k, p, g, leg), leg[2]) for leg in group if leg[2] < 2]

        def relay():
            clock.act(lambda: taken(ag_r.at[p, slot(k, g), 0], k, p, g, False))
            last = [ag_send(k, p, g, leg) for leg in group if leg[2] == 2]
            clock.done.add(("passed", k, p, g))
            clock.later(max([ready for ready, _ in due] + last), (), finish)

        def finish():
            clock.act(lambda: taken(ag_r.at[p, slot(k, g), 1], k, p, g, True))
            clock.done.add(("ag", k, p, g))
            if (k, g) == (2, 0):
                ag_start(1, p, 1)
                ag_start(0, p, 1)
            elif k == 1:
                ag_start(0, p, 2 + g)

        clock.later(max(ready for ready, stage in due if stage == 0), (), relay)

    def rs_place(k, p, g, h, side, stage):
        one, rest = pl.ds(0, 1), pl.ds(1, 3)
        a, b = (rest if g & 2 else one), (rest if g & 1 else one)
        ref = ((rx1, rx2, rx3) if stage == 0 else (fl1, fl2, fl3) if side > 0 else (fr1, fr2, fr3))[k]
        return ref.at[p, h, a, b] if k == 0 else ref.at[p, h, b] if k == 1 else ref.at[p, h]

    def rs_send(k, p, g, leg):
        h, side, stage = leg

        def copy():
            src = region(ps, p, h, k, g, 2 if stage == 0 else side % 4)
            dst = rs_place(k, p, g, h, side, stage)
            return remote(src, dst, rs_s.at[k], rs_r.at[p, slot(k, g), min(stage, 1)], near(AXES[p][k], side))

        return clock.send(copy, size(g, leg), (AXES[p][k], side))

    def add_into(k, p, g, q, h, sources):
        wide = 3 if g & 1 else 1
        dst = region(ps, p, h, k, g, q)
        refs = [rs_place(k, p, g, h, side, stage) for side, stage in sources]

        def one(n, carry):
            index = (lax.div(n, wide), lax.rem(n, wide)) if k == 0 else (n,)
            total = dst[index].astype(F32)
            for ref in refs:
                total = total + ref[index].astype(F32)
            dst[index] = total.astype(BF16)
            return carry

        lax.fori_loop(0, BLOCKS[g], one, 0)

    def rs_start(k, p, g):
        group = legs(k, g, -1)
        due = [(rs_send(k, p, g, leg), leg[2]) for leg in group if leg[2] < 2]

        def relay():
            clock.act(lambda: taken(rs_r.at[p, slot(k, g), 0], k, p, g, False))
            last = []
            for leg in group:
                if leg[2] < 2:
                    continue
                for h in (0, 1) if leg[0] is BOTH else (leg[0],):
                    clock.act(lambda h=h, side=leg[1]: add_into(k, p, g, side % 4, h, ((side, 0),)))
                    clock.now += 0.03 * BLOCKS[g]
                last.append(rs_send(k, p, g, leg))
            clock.later(max([ready for ready, _ in due] + last), (("fwd", p, 0),), finish)
            if k == 0:
                for follower in {3: (2, 1), 2: (0,)}.get(g, ()):
                    rs_start(0, p, follower)

        def finish():
            clock.act(lambda: taken(rs_r.at[p, slot(k, g), 1], k, p, g, True))
            for h in range(2):
                clock.act(lambda h=h: add_into(k, p, g, 0, h, ((1, 1), (-1, 1))))
                clock.now += 0.03 * BLOCKS[g]
            done = clock.done
            done.add(("rs", k, p, g))
            if k == 0 and g & 2:
                rs_start(1, p, g & 1)
            if (k, g) in ((0, 1), (1, 1)) and done.issuperset((("rs", 0, p, 1), ("rs", 1, p, 1))):
                rs_start(2, p, 0)
            if done.issuperset(("rs", m, p, 0) for m in range(3)):
                def set_down():
                    for h in range(2):
                        mst[64 * h:64 * h + 64, 256 * p:256 * (p + 1)] = ps[p, h, 0, 0, 0]

                clock.act(set_down)
                done.add(("sum", p))

        clock.later(max(ready for ready, stage in due if stage == 0), (), relay)

    own = go.at[:, :, 0, 0, 0]
    pltpu.make_async_copy(own, own, gl).wait()
    clock.run("first")
    for p in range(3):
        ag_start(2, p, 0)
    clock.emit("first")
    def info_copy(axis, n):
        q, side = ((3, 1), (1, -1), (2, 2))[n]
        src, dst = (info.at[0, 0], info.at[0, q]) if axis == "y" else (info.at[0], info.at[q])
        i = ("y", "z").index(axis) * 3 + n
        return remote(src, dst, in_s.at[i], in_r.at[i], near(axis, side))

    def info_start(axis):
        due = [clock.send(lambda n=n: info_copy(axis, n), 0.1, (axis, (1, -1, 1)[n])) for n in range(3)]

        def finish():
            def all_in():
                for n in range(3):
                    info_copy(axis, n).wait_recv()

            clock.act(all_in)
            clock.done.add(("info", axis))
            if axis == "y":
                info_start("z")

        clock.later(max(due) + 1.0, (), finish)

    rt_local.wait()
    gt_local.wait()
    row = lax.broadcasted_iota(jnp.int32, (8, 128), 0)
    eid = x * 2 + lax.rem(row, 2)
    is0 = rv_i[0:1, :] == eid
    is1 = rv_i[1:2, :] == eid
    gate = jnp.where(is0, rv_g[0:1, :], 0.0) + jnp.where(is1, rv_g[1:2, :], 0.0)
    named = jnp.where(is0, 1.0, 0.0) + jnp.where(is1, 1.0, 0.0)
    before = jnp.where(
        lax.broadcasted_iota(jnp.int32, (128, 128), 0) < lax.broadcasted_iota(jnp.int32, (128, 128), 1), 1.0, 0.0
    )
    rank = dot(jnp.concatenate([named, named], axis=0).astype(BF16), before.astype(BF16))[0:8, :]
    info[0, 0] = jnp.where(row < 2, jnp.where(named > 0.5, rank, -1.0), gate)

    clock.run("second")
    info_start("y")
    for k in (1, 0):
        for p in range(3):
            ag_start(k, p, 0)
    clock.emit("second")

    def h_copy(e, device):
        return remote(hid, hv.at[:, pl.ds(pl.multiple_of(e * 64, 64), 64), :], h_s, h_r, device)

    def w_copy(b, e, of, device):
        cols = pl.ds(pl.multiple_of(b * 1536 + of * 768, 128), 768)
        rows = pl.ds(pl.multiple_of(e * 512, 512), 512)
        return remote(w.at[:, cols], wv.at[rows, pl.ds(b * 768, 768)], w_s, w_r, device)

    h_copy(c, partner).start()
    for b in range(4):
        w_copy(b, c, oc, partner).start()

    def turning(e):
        def turn(n, carry):
            pair = jnp.concatenate([hv[n * 2, e * 64:e * 64 + 64, :], hv[n * 2 + 1, e * 64:e * 64 + 64, :]], axis=0)
            ht[e, :, pl.ds(pl.multiple_of(n * 128, 128), 128)] = pair.T
            return carry

        lax.fori_loop(0, 8, turn, 0)

    place = lax.broadcasted_iota(jnp.int32, (128, 128), 0).astype(F32)
    lane = lax.broadcasted_iota(jnp.int32, (128, 128), 1)

    def mix(d, carry):
        zz, yy = lax.div(d, 4), lax.rem(d, 4)
        part = info[rel("z", zz), rel("y", yy)]
        first = jnp.where(part[0:1, :] == place, part[2:3, :], 0.0)
        second = jnp.where(part[1:2, :] == place - 64.0, part[3:4, :], 0.0)
        spread = first + second
        gm[d] = spread.astype(BF16)
        turned = spread.T
        rows = hv[d]
        mv[zz, yy, :, 0:512] = dot(jnp.where(lane < 64, turned, 0.0).astype(BF16), rows).astype(BF16)
        mv[zz, yy, :, 512:1024] = dot(jnp.where(lane < 64, 0.0, turned).astype(BF16), rows).astype(BF16)
        return carry

    def mixing(m, carry):
        clock.emit(*[("mix", v) for v in range(4)], index=m)
        return lax.fori_loop(4 * m, 4 * m + 4, mix, carry)

    def forward(p):
        def step(s, carry):
            clock.emit(*[("fwd", p, v) for v in range(8)], index=s)
            j = lax.rem(6 - lax.div(s, 2), 4)
            chunk_at = at(AXES[p][0], j)

            def tile(n, carry):
                if p == 0:
                    left = mv[at("z", n)]
                    cols = chunk_at * 768
                elif p == 1:
                    left = mv[:, chunk_at]
                    cols = n * 768 + 256
                else:
                    left = mv[chunk_at]
                    cols = n * 768 + 512
                right = wv[:, pl.ds(pl.multiple_of(cols, 128), 256)]
                out = dot(left.reshape(512, 1024), right).astype(BF16)
                for q in range(4):
                    for h in range(2):
                        piece = out[128 * q + 64 * h:128 * q + 64 * h + 64]
                        if p == 0:
                            ps[p, h, j, rel("y", q), n] = piece
                        elif p == 1:
                            ps[p, h, j, rel("z", q), rel("x", n)] = piece
                        else:
                            ps[p, h, j, rel("x", n), rel("y", q)] = piece
                return carry

            start = 2 * lax.rem(s, 2)
            return lax.fori_loop(start, start + 2, tile, carry)

        lax.fori_loop(0, 8, step, 0)

    def gw_out(b, mine):
        e = c if mine else oc
        cols = pl.ds(pl.multiple_of(b * 1536 + c * 768, 128), 768)
        if mine:
            return pltpu.make_async_copy(gws.at[e], gwt.at[:, cols], gwl)
        return remote(gws.at[e], gwt.at[:, cols], gw_s, gw_r, partner)

    def routed(b):
        def one(d, carry):
            zz, yy = lax.div(d, 4), lax.rem(d, 4)
            left = gm[d]
            start = pl.multiple_of(d * 64, 64)
            rx, ry, rz = rel("x", b), rel("y", yy), rel("z", zz)
            for p, (i, j, k) in enumerate(((rx, ry, rz), (ry, rz, rx), (rz, rx, ry))):
                right = jnp.concatenate([go[p, 0, i, j, k], go[p, 1, i, j, k]], axis=0)
                out = dot(left, right).astype(BF16)
                rv[0, pl.ds(start, 64), 256 * p:256 * (p + 1)] = out[0:64]
                rv[1, pl.ds(start, 64), 256 * p:256 * (p + 1)] = out[64:128]
            return carry

        def some(m, carry):
            clock.emit(*[("routed", v) for v in range(8)], index=2 * b + m)
            return lax.fori_loop(8 * m, 8 * m + 8, one, carry)

        lax.fori_loop(0, 2, some, 0)

    def weight_grad(b):
        def one(i, carry):
            clock.emit(*[("weight", v) for v in range(24)], index=6 * b + i)
            last = b - 1

            @pl.when(jnp.logical_and(b > 0, i == 0))
            def _():
                gw_out(last, False).wait_send()

            @pl.when(jnp.logical_and(b > 0, i == 3))
            def _():
                gw_out(last, True).wait()

            mine = lax.div(i, 3)
            e = mine * c + (1 - mine) * oc
            cols = pl.ds(pl.multiple_of(lax.rem(i, 3) * 256, 256), 256)
            gws[e, :, cols] = dot(ht[e], rv[e, :, cols]).astype(BF16)

            @pl.when(i == 2)
            def _():
                gw_out(b, False).start()

            @pl.when(i == 5)
            def _():
                gw_out(b, True).start()

            return carry

        lax.fori_loop(0, 6, one, 0)

    gh_copy = remote(hv.at[:, 0:64, :], ghr, gh_s, gh_r, partner)

    def pack(d, carry):
        hv[d, 0:64, :] = acc[oc, pl.ds(pl.multiple_of(d * 64, 64), 64), :].astype(BF16)
        return carry

    def close(d, carry):
        own = acc[c, pl.ds(pl.multiple_of(d * 64, 64), 64), :]
        hv[d, 64:128, :] = (own + ghr[d].astype(F32)).astype(BF16)
        return carry

    def hidden_grad(b):
        right_cols = pl.ds(pl.multiple_of(b * 768, 128), 768)

        def some(i, carry):
            clock.emit(*[("hidden", v) for v in range(16)], index=4 * b + i)

            @pl.when(jnp.logical_and(b == 3, i == 2))
            def _():
                lax.fori_loop(0, 16, pack, 0)
                gh_copy.start()

            mine = lax.div(i, 2)
            e = mine * c + (1 - mine) * oc

            def one(n, carry):
                rows = pl.ds(pl.multiple_of(n * 256, 256), 256)
                right = wv[pl.ds(pl.multiple_of(e * 512, 512), 512), right_cols]
                out = lax.dot_general(rv[e, rows, :], right, DN_T, preferred_element_type=F32)
                acc[e, rows, :] = acc[e, rows, :] + out
                return carry

            start = 2 * lax.rem(i, 2)
            return lax.fori_loop(start, start + 2, one, carry)

        lax.fori_loop(0, 4, some, 0)

    def backward(b, carry):
        routed(b)
        hidden_grad(b)
        weight_grad(b)
        return carry

    def clear(n, carry):
        rows = pl.ds(pl.multiple_of(n * 64, 64), 64)
        for e in range(2):
            acc[e, rows, :] = jnp.zeros((64, 512), F32)
        return carry

    clock.now += 4.0
    clock.run("turn", 2.0)
    clock.run("info", 0.0, [("info", "z")])
    for m in range(4):
        clock.run(("mix", m), 0.75)
    for p in range(3):
        for v in range(8):
            clock.run(("fwd", p, v), FWD)
        clock.done.add(("fwd", p, 0))
        clock.later(clock.now, [("passed", 0, p, g) for g in range(4)], lambda p=p: rs_start(0, p, 3))
    clock.run("gathered", 0.0, [("ag", 0, p, g) for p in range(3) for g in range(4)])
    for b in range(4):
        for m in range(2):
            clock.run(("routed", 2 * b + m), ROUTED)
        for i in range(4):
            clock.run(("hidden", 4 * b + i), HIDDEN)
        for i in range(6):
            clock.run(("weight", 6 * b + i), WEIGHT)
    clock.run("close", 0.5)
    clock.run("summed", 0.0, [("sum", p) for p in range(3)])

    h_local.wait()
    h_copy(oc, partner).wait_recv()
    clock.emit("turn")
    lax.fori_loop(0, 16, clear, 0)
    turning(0)
    turning(1)
    clock.emit("info")
    lax.fori_loop(0, 4, mixing, 0)
    mine, theirs = (wv.at[pl.ds(pl.multiple_of(e * 512, 512), 512)] for e in (c, oc))
    pltpu.make_async_copy(mine, mine, wl).wait()
    remote(theirs, theirs, w_s, w_r, partner).wait_recv()
    for p in range(3):
        forward(p)
    clock.emit("gathered")
    lax.fori_loop(0, 4, backward, 0)
    clock.emit("close")
    gh_copy.wait_recv()
    lax.fori_loop(0, 16, close, 0)
    gh_out = pltpu.make_async_copy(hv.at[:, 64:128, :], ghid, outl.at[0])
    gh_out.start()
    clock.emit("summed")
    assert not clock.places and not clock.pending
    mixed_out = pltpu.make_async_copy(mst, mixed, outl.at[1])
    mixed_out.start()

    for k, all_sent in enumerate((go.at[:, :, 0:3], go.at[:, :, 0, 0:3], go.at[:, :, 0, 0, 0:3])):
        for sem in (ag_s.at[k], rs_s.at[k]):
            remote(all_sent, all_sent, sem, sem, partner).wait_send()
    for axis in "yz":
        for n in range(3):
            info_copy(axis, n).wait_send()
    h_copy(c, partner).wait_send()
    remote(mine, mine, w_s, w_r, partner).wait_send()
    landed = gwt.at[:, 0:3072]
    remote(landed, landed, gw_s, gw_r, partner).wait_recv()
    gw_out(3, False).wait_send()
    gw_out(3, True).wait()
    gh_copy.wait_send()
    gh_out.wait()
    mixed_out.wait()


def hand_on(a, b, c, a_out, b_out, c_out, av, bv, cv, isem, osem):
    steps = [(a, av, a_out, None), (b, bv, b_out, None)] + [(c, cv, c_out, n) for n in range(8)]
    copies = []
    for i, (src, mid, dst, n) in enumerate(steps):
        if n is not None:
            rows = pl.ds(64 * n, 64)
            src, mid, dst = src.at[rows], mid.at[rows], dst.at[rows]
        copies.append(
            (pltpu.make_async_copy(src, mid, isem.at[i]), pltpu.make_async_copy(mid, dst, osem.at[i]))
        )
    for first, _ in copies:
        first.start()
    for first, second in copies:
        first.wait()
        second.start()
    for _, second in copies:
        second.wait()


def body(hidden, down_weight, grad_out, routing, gates):
    dma = pltpu.SemaphoreType.DMA
    sums = []
    for lead in ((4, 4), (4,), ()):
        sums += [pltpu.VMEM((3, 2, *(lead or (1,)), 64, 256), BF16)] * 3
    anywhere = pl.BlockSpec(memory_space=pl.ANY)
    outs = (
        jax.ShapeDtypeStruct((128, 768), BF16),
        jax.ShapeDtypeStruct((16, 64, 512), BF16),
        jax.ShapeDtypeStruct((512, 6144), BF16),
    )
    results = pl.pallas_call(
        kernel,
        out_shape=outs,
        in_specs=[anywhere] * 5,
        out_specs=(anywhere, anywhere, anywhere),
        scratch_shapes=[
            pltpu.VMEM((3, 2, 4, 4, 4, 64, 256), BF16),
            pltpu.VMEM((3, 2, 4, 4, 4, 64, 256), BF16),
            *sums,
            pltpu.VMEM((1024, 3072), BF16),
            pltpu.VMEM((16, 128, 512), BF16),
            pltpu.VMEM((2, 512, 1024), BF16),
            pltpu.VMEM((4, 4, 128, 1024), BF16),
            pltpu.VMEM((2, 1024, 768), BF16),
            pltpu.VMEM((2, 1024, 512), F32),
            pltpu.VMEM((2, 512, 768), BF16),
            pltpu.VMEM((16, 64, 512), BF16),
            pltpu.VMEM((16, 128, 128), BF16),
            pltpu.VMEM((4, 4, 8, 128), F32),
            pltpu.VMEM((128, 768), BF16),
            pltpu.VMEM((2, 128), jnp.int32),
            pltpu.VMEM((2, 128), F32),
            dma((3,)), dma((3, 7, 2)), dma((3,)), dma((3, 7, 2)),
            dma(()), dma(()), dma(()), dma(()), dma((6,)), dma((6,)),
            dma(()), dma(()), dma(()), dma(()),
            dma(()), dma(()), dma(()), dma(()), dma((2,)), dma((2,)),
        ],
        compiler_params=pltpu.CompilerParams(
            collective_id=0, has_side_effects=True, vmem_limit_bytes=67043328
        ),
    )(
        hidden.reshape(16, 64, 512),
        down_weight[0],
        grad_out,
        routing.T,
        gates.T,
    )
    mixed, ghid, gwt = pl.pallas_call(
        hand_on,
        out_shape=outs,
        in_specs=[anywhere] * 3,
        out_specs=(anywhere,) * 3,
        scratch_shapes=[pltpu.VMEM(out.shape, BF16) for out in outs] + [dma((10,)), dma((10,))],
        compiler_params=pltpu.CompilerParams(vmem_limit_bytes=67043328),
    )(*results)
    return mixed, ghid.reshape(1, 1024, 512), gwt[None]


def solution(mesh):
    return jax.shard_map(
        body,
        mesh=mesh,
        in_specs=(
            P("expert", None, "dp"),
            P("expert", "dp", None),
            P("dp", "expert"),
            P("dp", None),
            P("dp", None),
        ),
        out_specs=(P("dp", "expert"), P("expert", None, "dp"), P("expert", "dp", None)),
        check_vma=False,
    )
```

time: 116 us -> 112 us (0.966)
  Pallas kernels: 115 us -> 111 us
    pallas_call x1, Pallas kernels: 109 us -> 105 us  [body(): pl.pallas_call(kernel, out_shape=outs, in_specs=[anywhere] * 5, out_specs...]
where the time goes in v3:
time: 112 us
  Pallas kernels  111 us (99%)
    pallas_call x1, Pallas kernels, body(): pl.pallas_call(kernel, out_shape=outs, in_specs=[anywhere] * 5, out_specs...  105 us
    pallas_call x1, Pallas kernels, body(): pl.pallas_call(hand_on, out_shape=outs, in_specs=[anywhere] * 3, out_spec...  6.11 us

profile of v3, /device:TPU:1, one launch (start us, length us, event | category | flops | bytes accessed | tf_op | source)
XLA Modules:
  0.0 111.8 jit_solution(15587750477726040692)
XLA Ops:
  0.6 105.0 %shard_map.76 = (bf16[128,768]{1,0:T(8,128)(2,1)}, bf16[16,64,512]{2,1,0:T(8,128)(2,1)}, bf16[512,6144]{1,0:T(8,128)(2,1)}) custom-call(bf16[16,64,512]{2,1,0:T(8,128)(2,1)} %bitcast.7, bf16[512,6144]{1,0:T(8,128)(2,1)} %bitcast.6, bf16[128,768]{1,0:T(8,128)(2,1)} %gin.1, s32[2,128]{1,0:T(2,128)} %bitcast.8, f32[2,128]{1,0:T(2,128)} %bitcast.9), custom_call_target="tpu_custom_call" | custom-call | tf_op jit(solution)/shard_map/pallas_call | solution.py:584
  105.7 6.1 %shard_map.77 = (bf16[128,768]{1,0:T(8,128)(2,1)}, bf16[16,64,512]{2,1,0:T(8,128)(2,1)}, bf16[512,6144]{1,0:T(8,128)(2,1)}) custom-call(bf16[128,768]{1,0:T(8,128)(2,1)} %get-tuple-element.9.a, bf16[16,64,512]{2,1,0:T(8,128)(2,1)} %get-tuple-element.10.b, bf16[512,6144]{1,0:T(8,128)(2,1)} %get-tuple-element.11.c), custom_call_target="tpu_custom_call" | custom-call | tf_op jit(solution)/shard_map/pallas_call | solution.py:621
